TPU v7x, 32 devices: a whole 2x2x4 slice. The times are simulated.
32 devices in a mesh: dp: 8 (over y, x, core), mp: 4 (over z).
Axes of the slice: x: 2, y: 2, z: 4, core: 2. Of those that a mesh axis runs over, the one named last changes fastest.
Arguments:
- hidden_in: bfloat16 [16384, 2048], P('dp', 'mp')
- positions: int32 [16384], P('dp'), may hold values from 0 to 1023, as said below
- head_counts: int32 [4], replicated, may hold values from 4 to 6, as said below
- attention_gain: float32 [2048], P('mp'), may hold values from 0.5 to 1.5
- query_projection_weight: bfloat16 [2048, 1536], P(None, 'mp'), may hold values from -0.125 to 0.125
- key_weight: bfloat16 [2048, 320], replicated, may hold values from -0.125 to 0.125
- value_weight: bfloat16 [2048, 320], replicated, may hold values from -0.125 to 0.125
- query_gain: float32 [64], replicated, may hold values from 0.25 to 1.75
- key_gain: float32 [64], replicated, may hold values from 0.25 to 1.75
- output_weight: bfloat16 [1536, 2048], P(None, 'mp'), may hold values from -0.75 to 0.75
- feedforward_gain: float32 [2048], P('mp'), may hold values from 0.5 to 1.5
- gate_weight: bfloat16 [2048, 4096], P(None, 'mp'), may hold values from -0.125 to 0.125
- up_weight: bfloat16 [2048, 4096], P(None, 'mp'), may hold values from -0.125 to 0.125
- down_projection_weight: bfloat16 [4096, 2048], P('mp'), may hold values from -0.125 to 0.125
- cotangent: bfloat16 [16384, 2048], P('dp', 'mp'), may hold values from -6 to 6
Outputs:
- output: bfloat16 [16384, 2048], P('dp', 'mp')
- input_gradient: float32 [16384, 2048], P('dp', 'mp')
- attention_gain_gradient: float32 [2048], P('mp')
- query_weight_gradient: float32 [2048, 1536], P(None, 'mp')
- key_weight_gradient: float32 [2048, 320], replicated
- value_weight_gradient: float32 [2048, 320], replicated
- query_gain_gradient: float32 [64], replicated
- key_gain_gradient: float32 [64], replicated
- output_projection_gradient: float32 [1536, 2048], P(None, 'mp')
- feedforward_gain_gradient: float32 [2048], P('mp')
- gate_weight_gradient: float32 [2048, 4096], P(None, 'mp')
- up_weight_gradient: float32 [2048, 4096], P(None, 'mp')
- down_weight_gradient: float32 [4096, 2048], P('mp')
Inputs may be any that keep to these rules, and one draw needn't show every extreme that they name: `head_counts`: the counts sum to 20; index m's live heads follow those of lower indices; the largest count is 6 in every draw. `positions`: position ids count up by one along each sequence of 1024 tokens and restart at zero at its start and at up to three points inside it; the first sequence of all has no restart inside it.
All inputs are finite; a program needn't handle non-finite values.
Results may differ from a plain program's by a relative error of at most 0.025.
Values may be sent and summed in bfloat16 or wider, within the bound.
No kernel may reach another device: no remote copies, remote signals or barrier semaphores. Data moves between devices by JAX's collectives and lax.ppermute only.
A program may use at most 256 MiB of HBM per device.

v0:
```python
import math
import jax
import jax.numpy as jnp
from jax import lax
from jax.sharding import PartitionSpec as P

D = 2048
QH = 20
KVH = 5
HD = 64
LEN = 1024
BLK = 512
NBLK = 2
epsilon = 1e-05
rope_base = 10000.0
masked_score = -1e30


def rotary_tables(positions):
    half = HD // 2
    inverse = jnp.exp(-math.log(rope_base) * (2.0 * jnp.arange(half, dtype=jnp.float32)) / HD)
    angles = positions.astype(jnp.float32)[..., None] * inverse
    angles = jnp.concatenate([angles, angles], axis=-1)
    return (jnp.cos(angles), jnp.sin(angles))


def rotate(vectors, cosine, sine):
    half = vectors.shape[-1] // 2
    turned = jnp.concatenate([-vectors[..., half:], vectors[..., :half]], axis=-1)
    return vectors * cosine + turned * sine


def head_norm(vectors, gain):
    return vectors * lax.rsqrt(jnp.mean(vectors * vectors, axis=-1, keepdims=True) + epsilon) * gain


def inner(left_operand, right_operand):
    return lax.dot_general(
        left_operand, right_operand, (((0,), (0,)), ((), ())), preferred_element_type=jnp.float32
    )


def against(left_operand, right_operand):
    return lax.dot_general(
        left_operand, right_operand, (((1,), (1,)), ((), ())), preferred_element_type=jnp.float32
    )


def norm_forward(values, gain):
    squares = lax.psum(jnp.sum(values * values, axis=1), "mp")
    rms = lax.rsqrt(squares / D + epsilon)[:, None]
    normed = (values * rms * gain).astype(jnp.bfloat16)
    return (rms, lax.all_gather(normed, "mp", axis=1, tiled=True))


def norm_backward(values, rms, gain, normed_grad):
    weighted = normed_grad * gain
    dotted = lax.psum(jnp.sum(weighted * values, axis=1), "mp")[:, None]
    grad = weighted * rms - values * (rms * rms * rms) * dotted / D
    gain_grad = jnp.sum(normed_grad * values * rms, axis=0)
    return (grad, gain_grad)


def spread_sum(terms):
    return lax.psum_scatter(
        terms.astype(jnp.bfloat16), "mp", scatter_dimension=1, tiled=True
    ).astype(jnp.float32)


def on_device(
    hidden_in,
    positions,
    head_counts,
    attention_gain,
    query_projection_weight,
    key_weight,
    value_weight,
    query_gain,
    key_gain,
    output_weight,
    feedforward_gain,
    gate_weight,
    up_weight,
    down_projection_weight,
    cotangent,
):
    parts = lax.axis_size("mp")
    rank = lax.axis_index("mp")
    tokens = hidden_in.shape[0]
    share = hidden_in.shape[1]
    slots_here = query_projection_weight.shape[1] // HD
    seqs = tokens // LEN
    scale = 1.0 / math.sqrt(HD)
    ranks = jnp.arange(parts, dtype=jnp.int32)
    offset = jnp.sum(jnp.where(ranks < rank, head_counts, 0))
    count = jnp.sum(jnp.where(ranks == rank, head_counts, 0))
    within = jnp.arange(slots_here, dtype=jnp.int32)
    live = (within < count).astype(jnp.float32)
    groups = jnp.minimum((offset + within) // (QH // KVH), KVH - 1)
    choose = (groups[:, None] == jnp.arange(KVH, dtype=jnp.int32)[None, :]).astype(jnp.float32)
    choose_low = choose.astype(jnp.bfloat16)
    cosine, sine = rotary_tables(positions)

    def turn(raw, gain):
        heads = raw.reshape(tokens, -1, HD)
        return rotate(head_norm(heads, gain), cosine[:, None, :], sine[:, None, :])

    inputs = hidden_in.astype(jnp.float32)
    first_rms, normed_full = norm_forward(inputs, attention_gain)
    queries = jnp.dot(normed_full, query_projection_weight, preferred_element_type=jnp.float32)
    keys = jnp.dot(normed_full, key_weight, preferred_element_type=jnp.float32)
    values_low = jnp.dot(normed_full, value_weight, preferred_element_type=jnp.float32).astype(
        jnp.bfloat16
    )
    turned_queries, query_pull = jax.vjp(turn, queries, query_gain)
    turned_keys, key_pull = jax.vjp(turn, keys, key_gain)
    turned_queries = turned_queries.astype(jnp.bfloat16)
    turned_keys = turned_keys.astype(jnp.bfloat16)
    query_heads = jnp.transpose(turned_queries.reshape(seqs, LEN, slots_here, HD), (0, 2, 1, 3))
    key_heads = jnp.einsum(
        "hg,slgd->shld",
        choose_low,
        turned_keys.reshape(seqs, LEN, KVH, HD),
        preferred_element_type=jnp.float32,
    ).astype(jnp.bfloat16)
    value_heads = jnp.einsum(
        "hg,slgd->shld",
        choose_low,
        values_low.reshape(seqs, LEN, KVH, HD),
        preferred_element_type=jnp.float32,
    ).astype(jnp.bfloat16)
    query_blocks = jnp.moveaxis(query_heads.reshape(seqs, slots_here, NBLK, BLK, HD), 2, 0)
    starts = jnp.arange(NBLK, dtype=jnp.int32) * BLK
    cols = jnp.arange(LEN, dtype=jnp.int32)

    def block_scores(block, start):
        scores = (
            jnp.einsum("shid,shjd->shij", block, key_heads, preferred_element_type=jnp.float32)
            * scale
        )
        rows = start + jnp.arange(BLK, dtype=jnp.int32)
        allowed = cols[None, :] <= rows[:, None]
        return jnp.where(allowed, scores, masked_score)

    def attend_block(block_args):
        block, start = block_args
        scores = block_scores(block, start)
        peak = jnp.max(scores, axis=-1, keepdims=True)
        weights = jnp.exp(scores - peak)
        total = jnp.sum(weights, axis=-1, keepdims=True)
        probs = (weights / total).astype(jnp.bfloat16)
        result = jnp.einsum(
            "shij,shjd->shid", probs, value_heads, preferred_element_type=jnp.float32
        )
        return (result, (peak + jnp.log(total))[..., 0])

    mixed, row_totals = lax.map(attend_block, (query_blocks, starts))
    mixed = jnp.moveaxis(mixed, 0, 2).reshape(seqs, slots_here, LEN, HD).astype(jnp.bfloat16)
    mixed = mixed * live.astype(jnp.bfloat16)[None, :, None, None]
    mixed_local = jnp.transpose(mixed, (0, 2, 1, 3)).reshape(tokens, slots_here * HD)
    all_heads = lax.all_gather(mixed_local, "mp", axis=1, tiled=True)
    branch = jnp.dot(all_heads, output_weight, preferred_element_type=jnp.float32)
    middle = inputs + branch
    second_rms, second_normed_complete = norm_forward(middle, feedforward_gain)
    gate = jnp.dot(second_normed_complete, gate_weight, preferred_element_type=jnp.float32)
    up = jnp.dot(second_normed_complete, up_weight, preferred_element_type=jnp.float32)
    sigma = jax.nn.sigmoid(gate)
    swish = gate * sigma
    hidden = (swish * up).astype(jnp.bfloat16)
    down_terms = jnp.dot(hidden, down_projection_weight, preferred_element_type=jnp.float32)
    output = (
        middle
        + lax.psum_scatter(
            down_terms.astype(jnp.bfloat16), "mp", scatter_dimension=1, tiled=True
        ).astype(jnp.float32)
    ).astype(jnp.bfloat16)
    cotangent_full = lax.all_gather(cotangent, "mp", axis=1, tiled=True)
    down_grad = inner(hidden, cotangent_full)
    hidden_grad = against(cotangent_full, down_projection_weight)
    gate_grad = (hidden_grad * up * sigma * (1.0 + gate * (1.0 - sigma))).astype(jnp.bfloat16)
    up_grad = (hidden_grad * swish).astype(jnp.bfloat16)
    gate_weight_grad = inner(second_normed_complete, gate_grad)
    up_weight_grad = inner(second_normed_complete, up_grad)
    normed_two_grad = spread_sum(against(gate_grad, gate_weight) + against(up_grad, up_weight))
    middle_part, feedforward_gain_grad = norm_backward(
        middle, second_rms, feedforward_gain, normed_two_grad
    )
    middle_grad = cotangent.astype(jnp.float32) + middle_part
    branch_grad = middle_grad.astype(jnp.bfloat16)
    output_weight_grad = inner(all_heads, branch_grad)
    slot_terms = against(branch_grad, output_weight)
    mixed_grad = lax.psum_scatter(
        slot_terms.astype(jnp.bfloat16), "mp", scatter_dimension=1, tiled=True
    ).astype(jnp.float32)
    mixed_grad = (mixed_grad.reshape(tokens, slots_here, HD) * live[None, :, None]).astype(
        jnp.bfloat16
    )
    grad_heads = jnp.transpose(mixed_grad.reshape(seqs, LEN, slots_here, HD), (0, 2, 1, 3))
    grad_blocks = jnp.moveaxis(grad_heads.reshape(seqs, slots_here, NBLK, BLK, HD), 2, 0)

    def back_block(carry, block_args):
        key_total, value_total = carry
        block, grad_block, row_total, start = block_args
        scores = block_scores(block, start)
        probs = jnp.exp(scores - row_total[..., None])
        probs_low = probs.astype(jnp.bfloat16)
        prob_grad = jnp.einsum(
            "shid,shjd->shij", grad_block, value_heads, preferred_element_type=jnp.float32
        )
        delta = jnp.sum(probs * prob_grad, axis=-1, keepdims=True)
        score_grad = (probs * (prob_grad - delta)).astype(jnp.bfloat16)
        query_grad = (
            jnp.einsum("shij,shjd->shid", score_grad, key_heads, preferred_element_type=jnp.float32)
            * scale
        )
        key_total = (
            key_total
            + jnp.einsum("shij,shid->shjd", score_grad, block, preferred_element_type=jnp.float32)
            * scale
        )
        value_total = value_total + jnp.einsum(
            "shij,shid->shjd", probs_low, grad_block, preferred_element_type=jnp.float32
        )
        return ((key_total, value_total), query_grad)

    empty = jnp.zeros((seqs, slots_here, LEN, HD), jnp.float32)
    (key_slot_grad, value_slot_grad), query_block_grads = lax.scan(
        back_block, (empty, empty), (query_blocks, grad_blocks, row_totals, starts)
    )
    query_rot_grad = jnp.moveaxis(query_block_grads, 0, 2).reshape(seqs, slots_here, LEN, HD)
    query_rot_grad = jnp.transpose(query_rot_grad, (0, 2, 1, 3)).reshape(tokens, slots_here, HD)
    key_rot_grad = jnp.einsum("hg,shld->slgd", choose, key_slot_grad).reshape(tokens, KVH, HD)
    value_grad = jnp.einsum("hg,shld->slgd", choose, value_slot_grad).reshape(tokens, KVH * HD)
    query_unrotated_gradient, query_gain_part = query_pull(query_rot_grad)
    key_raw_grad, key_gain_part = key_pull(key_rot_grad)
    summed = (
        lax.psum(key_raw_grad.astype(jnp.bfloat16), "mp").astype(jnp.float32),
        lax.psum(value_grad.astype(jnp.bfloat16), "mp").astype(jnp.float32),
        lax.psum(query_gain_part.astype(jnp.bfloat16), "mp").astype(jnp.float32),
        lax.psum(key_gain_part.astype(jnp.bfloat16), "mp").astype(jnp.float32),
    )
    keys_low = summed[0].astype(jnp.bfloat16)
    values_grad_low = summed[1].astype(jnp.bfloat16)
    queries_low = query_unrotated_gradient.astype(jnp.bfloat16)
    query_weight_grad = inner(normed_full, queries_low)
    key_weight_grad = inner(normed_full, keys_low)
    value_weight_grad = inner(normed_full, values_grad_low)
    normed_grad = spread_sum(against(queries_low, query_projection_weight))
    key_rows = lax.dynamic_slice_in_dim(key_weight, rank * share, share, 0)
    value_rows = lax.dynamic_slice_in_dim(value_weight, rank * share, share, 0)
    normed_grad = normed_grad + against(keys_low, key_rows) + against(values_grad_low, value_rows)
    input_part, attention_gain_grad = norm_backward(inputs, first_rms, attention_gain, normed_grad)
    input_gradient = middle_grad + input_part
    totals = (
        lax.psum(attention_gain_grad.astype(jnp.bfloat16), "dp").astype(jnp.float32),
        lax.psum(query_weight_grad.astype(jnp.bfloat16), "dp").astype(jnp.float32),
        lax.psum(key_weight_grad.astype(jnp.bfloat16), "dp").astype(jnp.float32),
        lax.psum(value_weight_grad.astype(jnp.bfloat16), "dp").astype(jnp.float32),
        lax.psum(summed[2].astype(jnp.bfloat16), "dp").astype(jnp.float32),
        lax.psum(summed[3].astype(jnp.bfloat16), "dp").astype(jnp.float32),
        lax.psum(output_weight_grad.astype(jnp.bfloat16), "dp").astype(jnp.float32),
        lax.psum(feedforward_gain_grad.astype(jnp.bfloat16), "dp").astype(jnp.float32),
        lax.psum(gate_weight_grad.astype(jnp.bfloat16), "dp").astype(jnp.float32),
        lax.psum(up_weight_grad.astype(jnp.bfloat16), "dp").astype(jnp.float32),
        lax.psum(down_grad.astype(jnp.bfloat16), "dp").astype(jnp.float32),
    )
    return (
        output,
        input_gradient,
        totals[0],
        totals[1],
        totals[2],
        totals[3],
        totals[4],
        totals[5],
        totals[6],
        totals[7],
        totals[8],
        totals[9],
        totals[10],
    )


def solution(mesh):
    in_specs = (
        P("dp", "mp"),
        P("dp"),
        P(),
        P("mp"),
        P(None, "mp"),
        P(),
        P(),
        P(),
        P(),
        P(None, "mp"),
        P("mp"),
        P(None, "mp"),
        P(None, "mp"),
        P("mp", None),
        P("dp", "mp"),
    )
    out_specs = (
        P("dp", "mp"),
        P("dp", "mp"),
        P("mp"),
        P(None, "mp"),
        P(),
        P(),
        P(),
        P(),
        P(None, "mp"),
        P("mp"),
        P(None, "mp"),
        P(None, "mp"),
        P("mp", None),
    )
    return jax.shard_map(
        on_device, mesh=mesh, in_specs=in_specs, out_specs=out_specs, check_vma=False
    )
```

profile of v0, /device:TPU:0, one launch (start us, length us, event | category | flops | bytes accessed | tf_op | source)
XLA Modules:
  0.0 2038.4 jit_solution(6352952060460513605)
XLA Ops:
  13.3 13.7 psum.133
  43.9 135.8 %all-gather.5.cloned.1.call-done = bf16[2048,2048]{0,1:T(8,128)(2,1)} async-done(((bf16[2048,512]{0,1:T(8,128)(2,1)}), bf16[2048,2048]{0,1:T(8,128)(2,1)}) %all-gather.5.cloned.1.call-update) | async-done | bytes 8388624 | tf_op jit(solution)/shard_map/all_gather | solution.py:53
  265.4 75.8 %while.30 = (s32[]{:T(128)}, bf16[2,2,6,512,64]{3,4,2,1,0:T(8,128)(2,1)}, f32[2,2,6,512]{3,2,1,0:T(8,128)S(1)}, s32[2]{0:T(128)S(1)}, bf16[2,2,6,512,64]{3,4,2,1...) while((s32[]{:T(128)}, ...), condition=%wide.region_8.9_spmd.clone.clone, body=%wide.region_5.8_spmd.clone.sunk.clone | while | flops 1686628864 | bytes 190279856 | solution.py:157
  267.4 12.2 fusion.187
  279.6 12.3 fusion.188
  305.2 12.2 fusion.187
  317.4 12.3 fusion.188
  347.0 113.7 %all-gather.7.cloned.1.call-done = bf16[2048,1536]{0,1:T(8,128)(2,1)} async-done(((bf16[2048,384]{0,1:T(8,128)(2,1)}), bf16[2048,1536]{0,1:T(8,128)(2,1)}) %all-gather.7.cloned.1.call-update) | async-done | bytes 6291472 | tf_op jit(solution)/shard_map/all_gather | solution.py:161
  482.3 148.5 %all-gather.9.cloned.1.call-done = bf16[2048,2048]{0,1:T(8,128)(2,1)} async-done(((bf16[2048,512]{0,1:T(8,128)(2,1)}), bf16[2048,2048]{0,1:T(8,128)(2,1)}) %all-gather.9.cloned.1.call-update) | async-done | bytes 8388624 | tf_op jit(solution)/shard_map/all_gather | solution.py:53
  630.8 14.9 fusion.109
  657.3 122.8 %all-gather.11.cloned.1.call-done = bf16[2048,2048]{1,0:T(8,128)(2,1)} async-done(((bf16[2048,512]{1,0:T(8,128)(2,1)}), bf16[2048,2048]{1,0:T(8,128)(2,1)}) %all-gather.11.cloned.1.call-update) | async-done | bytes 8388624 | tf_op jit(solution)/shard_map/all_gather | solution.py:177
  780.1 23.6 %multiply_convert_fusion.1 = (bf16[2048,1024]{1,0:T(8,128)(2,1)}, bf16[2048,1024]{1,0:T(8,128)(2,1)}, bf16[2048,1024]{1,0:T(8,128)(2,1)}) fusion(f32[2048,1024]{1,0:T(8,128)} %fusion.108, f32[2048,1024]{1,0:T(8,128)} %fusion.109, bf16[2048,2048]{1,0:T(8,128)(2,1)} %all-gather.11.cloned.1.call-done, bf16[1024,2048]{1,0:T(8,128)(2,1)} %param.32), kind=kOutput, calls=%fused_computation.53 | convolution fusion | flops 8621391872 | bytes 41943040 | tf_op jit(solution)/shard_map/dot_general | solution.py:44
  803.8 15.4 fusion.110
  819.2 14.4 add_convert_fusion
  833.6 14.0 convolution_convert_fusion.2
  851.6 124.8 %reduce-scatter.9.cloned.1.call-done = bf16[2048,512]{0,1:T(8,128)(2,1)} async-done(((bf16[2048,2048]{0,1:T(8,128)(2,1)}), bf16[2048,512]{0,1:T(8,128)(2,1)}) %reduce-scatter.9.cloned.1.call-update) | async-done | bytes 2097168 | tf_op jit(solution)/shard_map/reduce_scatter | solution.py:65
  992.7 131.9 %reduce-scatter.7.cloned.1.call-done = bf16[2048,512]{0,1:T(8,128)(2,1)} async-done(((bf16[2048,2048]{0,1:T(8,128)(2,1)}), bf16[2048,512]{0,1:T(8,128)(2,1)}) %reduce-scatter.7.cloned.1.call-update) | async-done | bytes 2097168 | tf_op jit(solution)/shard_map/reduce_scatter | solution.py:173
  1150.4 14.7 convolution_convert_fusion.3
  1165.1 12.8 convolution_convert_fusion.4
  1193.4 64.9 %reduce-scatter.13.cloned.1.call-done = bf16[384,2048]{1,0:T(8,128)(2,1)} async-done(((bf16[1536,2048]{1,0:T(8,128)(2,1)}), bf16[384,2048]{1,0:T(8,128)(2,1)}) %reduce-scatter.13.cloned.1.call-update) | async-done | bytes 1572880
  1280.8 164.1 %while.31 = (s32[]{:T(128)}, f32[2,6,1024,64]{2,3,1,0:T(8,128)}, f32[2,6,1024,64]{2,3,1,0:T(8,128)}, f32[2,2,6,512,64]{3,4,2,1,0:T(8,128)}, s32[2]{0:T(128)S(1)}...) while((s32[]{:T(128)}, f32[2,6,1024,64]{2,3,1,0:T(8,128)}, ...), condition=%wide.region_19.20_spmd.clone.clone, body=%wide.region_17.19_spmd.clone.sunk.clone | while | flops 4125747712 | bytes 278057216 | solution.py:227
  1294.5 13.4 select_add_fusion.7
  1307.9 18.2 multiply_reduce_fusion.10
  1326.1 17.3 multiply_convert_fusion.8
  1374.9 14.3 select_add_fusion.7
  1389.2 18.2 multiply_reduce_fusion.10
  1407.4 17.3 multiply_convert_fusion.8
  1491.8 91.7 %all-reduce.13.cloned.1.call-done = (bf16[2048,320]{0,1:T(8,128)(2,1)}, bf16[2048,320]{0,1:T(8,128)(2,1)}) async-done(((bf16[2048,320]{0,1:T(8,128)(2,1)}, bf16[2048,320]{0,1:T(8,128)(2,1)}), (bf16[2048,320]{0,1:T(8,128)(2,1)}, bf16[2048,320]{0,1:T(8,128)(2,1)})) %all-reduce.13.cloned.1.call-update) | async-done | bytes 2621456 | tf_op jit(solution)/shard_map/psum | solution.py:237
  1625.4 210.8 %all-reduce.11.cloned.1.call-done = (bf16[2048,384]{1,0:T(8,128)(2,1)}, bf16[2048,320]{0,1:T(8,128)(2,1)}, bf16[2048,320]{0,1:T(8,128)(2,1)}, bf16[1536,512]{1,0...) async-done(((bf16[2048,384]{1,0:T(8,128)(2,1)}, bf16[2048,320]{0,1:T(8,128)(2,1)}, bf16[2048,320]{0,1:T(8,128)(2,1)}, ...) | async-done | bytes 18350096 | tf_op jit(solution)/shard_map/psum | solution.py:256
  1860.1 122.8 %reduce-scatter.11.cloned.1.call-done = bf16[2048,512]{0,1:T(8,128)(2,1)} async-done(((bf16[2048,2048]{0,1:T(8,128)(2,1)}), bf16[2048,512]{0,1:T(8,128)(2,1)}) %reduce-scatter.11.cloned.1.call-update) | async-done | bytes 2097168 | tf_op jit(solution)/shard_map/reduce_scatter | solution.py:65
  1990.7 13.5 all-reduce.4
  2006.3 11.7 psum.138
  (332 shorter events, 457.5 us)
Async XLA Ops:
  7.2 218.1 %copy-start = (bf16[2048,384]{1,0:T(8,128)(2,1)S(1)}, bf16[2048,384]{1,0:T(8,128)(2,1)}, u32[]{:S(2)}) copy-start(bf16[2048,384]{1,0:T(8,128)(2,1)} %param.23) | copy-start | bytes 4718596
  7.2 21.1 %copy-start.48 = (f32[512]{0:T(512)S(1)}, f32[512]{0:T(512)}, u32[]{:S(2)}) copy-start(f32[512]{0:T(512)} %param.22) | copy-start | bytes 6148
  7.2 172.6 %all-gather.5.cloned.1.call-start = ((), (), s32[]{:S(2)}) async-start(), calls=%async_computation.4 | async-start | bytes 10485760 | tf_op jit(solution)/shard_map/all_gather | solution.py:53
  31.7 148.1 %copy-start.43 = (bf16[2048,320]{0,1:T(8,128)(2,1)S(1)}, bf16[2048,320]{0,1:T(8,128)(2,1)}, u32[]{:S(2)}) copy-start(bf16[2048,320]{0,1:T(8,128)(2,1)} %param.25) | copy-start | bytes 3932164
  31.7 429.0 %all-gather.7.cloned.1.call-start = ((), (), s32[]{:S(2)}) async-start(), calls=%async_computation.5 | async-start | bytes 7864320 | tf_op jit(solution)/shard_map/all_gather | solution.py:161
  31.9 155.3 %copy-start.58 = (f32[32]{0:T(128)}, f32[32]{0:T(128)S(1)}, u32[]{:S(2)}) copy-start(f32[32]{0:T(128)S(1)} %multiply_exponential_fusion) | copy-start | bytes 388
  33.2 189.5 %copy-start.50 = (s32[6]{0:T(128)}, s32[6]{0:T(128)S(1)}, u32[]{:S(2)}) copy-start(s32[6]{0:T(128)S(1)} %fusion.101) | copy-start | bytes 76
  42.6 173.4 %copy-start.16 = (f32[2,1024,64]{1,0,2:T(2,128)}, f32[2,1024,64]{1,0,2:T(2,128)S(1)}, u32[]{:S(2)}) copy-start(f32[2,1024,64]{1,0,2:T(2,128)S(1)} %get-tuple-element.371) | copy-start | bytes 1572868
  267.4 24.5 %copy-start.9 = (bf16[2,6,1024,64]{2,3,1,0:T(8,128)(2,1)S(1)}, bf16[2,6,1024,64]{2,3,1,0:T(8,128)(2,1)}, u32[]{:S(2)}) copy-start(bf16[2,6,1024,64]{2,3,1,0:T(8,128)(2,1)} %get-tuple-element.557) | copy-start | bytes 4718596 | tf_op jit(solution)/shard_map/while
  279.6 15.4 copy-start.2
  305.2 24.5 %copy-start.9 = (bf16[2,6,1024,64]{2,3,1,0:T(8,128)(2,1)S(1)}, bf16[2,6,1024,64]{2,3,1,0:T(8,128)(2,1)}, u32[]{:S(2)}) copy-start(bf16[2,6,1024,64]{2,3,1,0:T(8,128)(2,1)} %get-tuple-element.557) | copy-start | bytes 4718596 | tf_op jit(solution)/shard_map/while
  345.3 115.4 %copy-start.67 = (bf16[1536,512]{1,0:T(8,128)(2,1)S(1)}, bf16[1536,512]{1,0:T(8,128)(2,1)}, u32[]{:S(2)}) copy-start(bf16[1536,512]{1,0:T(8,128)(2,1)} %param.28) | copy-start | bytes 4718596
  347.0 130.8 %copy-start.47 = (f32[512]{0:T(512)S(1)}, f32[512]{0:T(512)}, u32[]{:S(2)}) copy-start(f32[512]{0:T(512)} %param.29) | copy-start | bytes 6148
  347.0 283.8 %all-gather.9.cloned.1.call-start = ((), (), s32[]{:S(2)}) async-start(), calls=%async_computation.6 | async-start | bytes 10485760 | tf_op jit(solution)/shard_map/all_gather | solution.py:53
  481.7 298.4 %all-gather.11.cloned.1.call-start = ((), (), s32[]{:S(2)}) async-start(), calls=%async_computation.8 | async-start | bytes 10485760 | tf_op jit(solution)/shard_map/all_gather | solution.py:177
  482.3 494.1 %reduce-scatter.9.cloned.1.call-start = ((), (), s32[]{:S(2)}) async-start(), calls=%async_computation.9 | async-start | bytes 10485760 | tf_op jit(solution)/shard_map/reduce_scatter | solution.py:65
  803.8 15.4 copy-start.66
  803.8 15.4 copy-start.70
  833.6 291.0 %reduce-scatter.7.cloned.1.call-start = ((), (), s32[]{:S(2)}) async-start(), calls=%async_computation.7 | async-start | bytes 10485760 | tf_op jit(solution)/shard_map/reduce_scatter | solution.py:173
  847.7 410.7 %reduce-scatter.13.cloned.1.call-start = ((), (), s32[]{:S(2)}) async-start(), calls=%async_computation.11 | async-start | bytes 7864320
  1146.7 436.8 %all-reduce.13.cloned.1.call-start = ((), (), s32[]{:S(2)}) async-start(), calls=%async_computation.13 | async-start | bytes 5242880 | tf_op jit(solution)/shard_map/psum | solution.py:237
  1150.4 27.5 %slice-start.4 = ((s8[8388608]{0:T(1024)(128)(4,1)}), s8[4194304]{0:T(1024)(128)(4,1)S(1)}, s32[]{:S(2)}) async-start(s8[8388608]{0:T(1024)(128)(4,1)} %bitcast.239), calls=%async_computation.18 | async-start | bytes 8388608
  1165.1 23.3 %slice-start.6 = ((s8[6291456]{0:T(1024)(128)(4,1)}), s8[4194304]{0:T(1024)(128)(4,1)S(1)}, s32[]{:S(2)}) async-start(s8[6291456]{0:T(1024)(128)(4,1)} %bitcast.241), calls=%async_computation.20 | async-start | bytes 8388608
  1326.1 21.8 %copy-start.6 = (bf16[2,2,6,512,64]{3,4,2,1,0:T(8,128)(2,1)S(1)}, bf16[2,2,6,512,64]{3,4,2,1,0:T(8,128)(2,1)}, u32[]{:S(2)}) copy-start(bf16[2,2,6,512,64]{3,4,2,1,0:T(8,128)(2,1)} %get-tuple-element.583) | copy-start | bytes 4718596 | tf_op jit(solution)/shard_map/while
  1407.4 21.8 %copy-start.6 = (bf16[2,2,6,512,64]{3,4,2,1,0:T(8,128)(2,1)S(1)}, bf16[2,2,6,512,64]{3,4,2,1,0:T(8,128)(2,1)}, u32[]{:S(2)}) copy-start(bf16[2,2,6,512,64]{3,4,2,1,0:T(8,128)(2,1)} %get-tuple-element.583) | copy-start | bytes 4718596 | tf_op jit(solution)/shard_map/while
  1478.3 357.9 %all-reduce.11.cloned.1.call-start = ((), (), s32[]{:S(2)}) async-start(), calls=%async_computation.12 | async-start | bytes 36700160 | tf_op jit(solution)/shard_map/psum | solution.py:256
  1598.8 384.1 %reduce-scatter.11.cloned.1.call-start = ((), (), s32[]{:S(2)}) async-start(), calls=%async_computation.10 | async-start | bytes 10485760 | tf_op jit(solution)/shard_map/reduce_scatter | solution.py:65
  1855.6 127.3 %copy-start.33 = (bf16[2048,320]{0,1:T(8,128)(2,1)S(1)}, bf16[2048,320]{0,1:T(8,128)(2,1)}, u32[]{:S(2)}) copy-start(bf16[2048,320]{0,1:T(8,128)(2,1)} %get-tuple-element.349) | copy-start | bytes 3932164
  1855.6 127.3 %copy-start.41 = (f32[2048]{0:T(1024)S(1)}, f32[2048]{0:T(1024)}, u32[]{:S(2)}) copy-start(f32[2048]{0:T(1024)} %copy-done.40) | copy-start | bytes 24580
  1855.6 127.3 %copy-start.49 = (f32[512]{0:T(512)S(1)}, f32[512]{0:T(512)}, u32[]{:S(2)}) copy-start(f32[512]{0:T(512)} %param.22) | copy-start | bytes 6148
  1860.1 130.7 %copy-start.57 = (bf16[512]{0:T(512)(128)(2,1)S(1)}, bf16[512]{0:T(512)(128)(2,1)}, u32[]{:S(2)}) copy-start(bf16[512]{0:T(512)(128)(2,1)} %get-tuple-element.291) | copy-start | bytes 3076
  1860.1 158.0 %copy-start.46 = (f32[2048]{0:T(1024)S(1)}, f32[2048]{0:T(1024)}, u32[]{:S(2)}) copy-start(f32[2048]{0:T(1024)} %get-tuple-element.373) | copy-start | bytes 24580
  (65 other events, 342.0 us)
Sparse Core Ops, SparseCore 0:
  31.9 147.8 all-gather.4
  347.1 113.5 all-gather.6
  481.8 148.9 all-gather.8
  632.2 147.8 all-gather.10
  833.7 142.6 reduce-scatter.8
  979.2 145.3 reduce-scatter.6
  1146.8 111.4 reduce-scatter.12
  1478.4 105.0 all-reduce.12
  1598.9 237.2 all-reduce.10
  1838.4 144.4 reduce-scatter.10
where the time goes:
time: 2050 us; the launch traced here: 2040 us
  waiting for transfers between devices  1270 us (62%)
  matrix products  376 us (18%)
  other arithmetic  173 us (8%)
  local copies, waits for them, and re-layouts  134 us (7%)
  blocking collectives  69.5 us (3%)
    all_gather x2, waiting for transfers between devices, norm_forward(): return (rms, lax.all_gather(normed, 'mp', axis=1, tiled=True))  284 us
    reduce_scatter x2, waiting for transfers between devices, spread_sum(): lax.psum_scatter(terms.astype(jnp.bfloat16), 'mp', scatter_dimension=1, t...  248 us
    psum x1, waiting for transfers between devices, on_device(): lax.psum(query_weight_grad.astype(jnp.bfloat16), 'dp').astype(jnp.float32)  211 us
    reduce_scatter x1, waiting for transfers between devices, on_device(): lax.psum_scatter(down_terms.astype(jnp.bfloat16), 'mp', scatter_dimension...  132 us
    all_gather x1, waiting for transfers between devices, on_device(): cotangent_full = lax.all_gather(cotangent, 'mp', axis=1, tiled=True)  123 us
    all_gather x1, waiting for transfers between devices, on_device(): all_heads = lax.all_gather(mixed_local, 'mp', axis=1, tiled=True)  114 us
    psum x1, waiting for transfers between devices, on_device(): lax.psum(key_raw_grad.astype(jnp.bfloat16), 'mp').astype(jnp.float32)  91.7 us
    dot_general x7, matrix products, against(): lax.dot_general(left_operand, right_operand, (((1,), (1,)), ((), ())), pr...  77.7 us
  transfers between devices with their start and end apart: 10, of which 10 were waited for; matrix products, arithmetic and copies ran while one was open for 8% of the time, Pallas kernels for 0%

commit v1 on v0

--- a/solution.py
+++ b/solution.py
@@ -1,3 +1,4 @@
+import functools
 import math
 import jax
 import jax.numpy as jnp
@@ -14,6 +15,31 @@
 epsilon = 1e-05
 rope_base = 10000.0
 masked_score = -1e30
+
+
+def derive_the_points(row_data, ndim_at):
+    odd = list(row_data.shape[1:])
+    odd[ndim_at] *= row_data.shape[0]
+    return jnp.moveaxis(row_data, 0, ndim_at).reshape(odd)
+
+
+def name_tables(xx, bus_axis):
+    s_next = xx[None]
+    shares = lax.axis_size(bus_axis)
+    for dd in range(shares.bit_length() - 1):
+        reply = 1 << dd
+        newest = lax.ppermute(s_next, bus_axis, [(at, at ^ reply) for at in range(shares)])
+        extra = jnp.stack([s_next, newest])
+        moved = lax.axis_index(bus_axis) >> dd & 1
+        s_next = jnp.where(moved == 0, extra, extra[::-1]).reshape(-1, *xx.shape)
+    return s_next
+
+
+def shelves_check(local_x, incoming_x, row_dim):
+    return derive_the_points(name_tables(local_x, incoming_x), row_dim)
+
+
+launch_local_data_by_axis = functools.partial(shelves_check, incoming_x="mp", row_dim=1)
 
 
 def rotary_tables(positions):
@@ -158,7 +184,7 @@
     mixed = jnp.moveaxis(mixed, 0, 2).reshape(seqs, slots_here, LEN, HD).astype(jnp.bfloat16)
     mixed = mixed * live.astype(jnp.bfloat16)[None, :, None, None]
     mixed_local = jnp.transpose(mixed, (0, 2, 1, 3)).reshape(tokens, slots_here * HD)
-    all_heads = lax.all_gather(mixed_local, "mp", axis=1, tiled=True)
+    all_heads = launch_local_data_by_axis(mixed_local)
     branch = jnp.dot(all_heads, output_weight, preferred_element_type=jnp.float32)
     middle = inputs + branch
     second_rms, second_normed_complete = norm_forward(middle, feedforward_gain)

time: 2050 us -> 2120 us (1.034)
  waiting for transfers between devices: 1270 us -> 1330 us
    ppermute x0 -> x2, waiting for transfers between devices: none -> 171 us  [name_tables(): lax.ppermute(s_next, bus_axis, [(at, at ^ reply) for at in range(shares)])]
    all_gather x1 -> x0, waiting for transfers between devices: 114 us -> none  [on_device(): all_heads = lax.all_gather(mixed_local, 'mp', axis=1, tiled=True)]
    unnamed x162 -> x167, local copies, waits for them, and re-layouts: 52.8 us -> 51.2 us
    unnamed x11 -> x10, waiting for transfers between devices: 65.6 us -> 65.9 us
  transfers between devices with their start and end apart: 10 -> 11, of which waited for: 10 -> 11; matrix products, arithmetic and copies ran while one was open for 8% -> 7% of each run, Pallas kernels for 0% -> 0%
where the time goes in v1:
time: 2120 us; the launch traced here: 2110 us
  waiting for transfers between devices  1330 us (63%)
  matrix products  373 us (18%)
  other arithmetic  185 us (9%)
  local copies, waits for them, and re-layouts  140 us (7%)
  blocking collectives  69.5 us (3%)
    all_gather x2, waiting for transfers between devices, norm_forward(): return (rms, lax.all_gather(normed, 'mp', axis=1, tiled=True))  284 us
    reduce_scatter x2, waiting for transfers between devices, spread_sum(): lax.psum_scatter(terms.astype(jnp.bfloat16), 'mp', scatter_dimension=1, t...  248 us
    psum x1, waiting for transfers between devices, on_device(): lax.psum(query_weight_grad.astype(jnp.bfloat16), 'dp').astype(jnp.float32)  211 us
    ppermute x2, waiting for transfers between devices, name_tables(): lax.ppermute(s_next, bus_axis, [(at, at ^ reply) for at in range(shares)])  171 us
    reduce_scatter x1, waiting for transfers between devices, on_device(): lax.psum_scatter(down_terms.astype(jnp.bfloat16), 'mp', scatter_dimension...  132 us
    all_gather x1, waiting for transfers between devices, on_device(): cotangent_full = lax.all_gather(cotangent, 'mp', axis=1, tiled=True)  123 us
    psum x1, waiting for transfers between devices, on_device(): lax.psum(key_raw_grad.astype(jnp.bfloat16), 'mp').astype(jnp.float32)  91.7 us
    dot_general x7, matrix products, against(): lax.dot_general(left_operand, right_operand, (((1,), (1,)), ((), ())), pr...  77.5 us
  transfers between devices with their start and end apart: 11, of which 11 were waited for; matrix products, arithmetic and copies ran while one was open for 7% of the time, Pallas kernels for 0%

profile of v1, /device:TPU:0, one launch (start us, length us, event | category | flops | bytes accessed | tf_op | source)
XLA Modules:
  0.0 2111.0 jit_solution(4877429889131383470)
XLA Ops:
  13.4 13.7 psum.133
  44.0 135.8 %all-gather.4.cloned.1.call-done = bf16[2048,2048]{0,1:T(8,128)(2,1)} async-done(((bf16[2048,512]{0,1:T(8,128)(2,1)}), bf16[2048,2048]{0,1:T(8,128)(2,1)}) %all-gather.4.cloned.1.call-update) | async-done | bytes 8388624 | tf_op jit(solution)/shard_map/all_gather | solution.py:79
  265.5 75.5 %while.30 = (s32[]{:T(128)}, bf16[2,2,6,512,64]{3,4,2,1,0:T(8,128)(2,1)}, f32[2,2,6,512]{3,2,1,0:T(8,128)S(1)}, s32[2]{0:T(128)S(1)}, bf16[2,2,6,512,64]{3,4,2,1...) while((s32[]{:T(128)}, ...), condition=%wide.region_8.9_spmd.clone.clone, body=%wide.region_5.8_spmd.clone.sunk.clone | while | flops 1686628864 | bytes 190279856 | solution.py:183
  267.4 12.1 fusion.189
  279.5 12.3 fusion.190
  305.0 12.1 fusion.189
  317.1 12.3 fusion.190
  353.0 33.8 %collective-permute-done = bf16[1,2048,384]{1,2,0:T(8,128)(2,1)} collective-permute-done((bf16[1,2048,384]{1,2,0:T(8,128)(2,1)}, bf16[1,2048,384]{1,2,0:T(8,128)(2,1)}, u32[]{:S(2)}, u32[]{:S(2)}) %collective-permute-start) | collective-permute-done | bytes 1572896 | tf_op jit(solution)/shard_map/ppermute | solution.py:31
  393.2 137.5 %collective-permute-done.1 = bf16[2,2048,384]{1,2,0:T(8,128)(2,1)} collective-permute-done((bf16[2,2048,384]{1,2,0:T(8,128)(2,1)}, bf16[2,2048,384]{1,2,0:T(8,128)(2,1)}, u32[]{:S(2)}, u32[]{:S(2)}) %collective-permute-start.1) | collective-permute-done | bytes 3145760 | tf_op jit(solution)/shard_map/ppermute | solution.py:31
  555.2 148.3 %all-gather.6.cloned.1.call-done = bf16[2048,2048]{0,1:T(8,128)(2,1)} async-done(((bf16[2048,512]{0,1:T(8,128)(2,1)}), bf16[2048,2048]{0,1:T(8,128)(2,1)}) %all-gather.6.cloned.1.call-update) | async-done | bytes 8388624 | tf_op jit(solution)/shard_map/all_gather | solution.py:79
  703.5 14.9 fusion.111
  730.0 123.0 %all-gather.8.cloned.1.call-done = bf16[2048,2048]{1,0:T(8,128)(2,1)} async-done(((bf16[2048,512]{1,0:T(8,128)(2,1)}), bf16[2048,2048]{1,0:T(8,128)(2,1)}) %all-gather.8.cloned.1.call-update) | async-done | bytes 8388624 | tf_op jit(solution)/shard_map/all_gather | solution.py:203
  853.0 23.5 %multiply_convert_fusion.1 = (bf16[2048,1024]{1,0:T(8,128)(2,1)}, bf16[2048,1024]{1,0:T(8,128)(2,1)}, bf16[2048,1024]{1,0:T(8,128)(2,1)}) fusion(f32[2048,1024]{1,0:T(8,128)} %fusion.110, f32[2048,1024]{1,0:T(8,128)} %fusion.111, bf16[2048,2048]{1,0:T(8,128)(2,1)} %all-gather.8.cloned.1.call-done, bf16[1024,2048]{1,0:T(8,128)(2,1)} %param.32), kind=kOutput, calls=%fused_computation.54 | convolution fusion | flops 8621391872 | bytes 41943040 | tf_op jit(solution)/shard_map/dot_general | solution.py:70
  876.5 15.4 fusion.112
  891.9 14.4 add_convert_fusion
  906.4 14.0 convolution_convert_fusion.2
  924.3 124.8 %reduce-scatter.9.cloned.1.call-done = bf16[2048,512]{0,1:T(8,128)(2,1)} async-done(((bf16[2048,2048]{0,1:T(8,128)(2,1)}), bf16[2048,512]{0,1:T(8,128)(2,1)}) %reduce-scatter.9.cloned.1.call-update) | async-done | bytes 2097168 | tf_op jit(solution)/shard_map/reduce_scatter | solution.py:91
  1065.4 131.9 %reduce-scatter.7.cloned.1.call-done = bf16[2048,512]{0,1:T(8,128)(2,1)} async-done(((bf16[2048,2048]{0,1:T(8,128)(2,1)}), bf16[2048,512]{0,1:T(8,128)(2,1)}) %reduce-scatter.7.cloned.1.call-update) | async-done | bytes 2097168 | tf_op jit(solution)/shard_map/reduce_scatter | solution.py:199
  1223.0 14.5 convolution_convert_fusion.3
  1237.5 12.9 convolution_convert_fusion.4
  1265.9 65.1 %reduce-scatter.13.cloned.1.call-done = bf16[384,2048]{1,0:T(8,128)(2,1)} async-done(((bf16[1536,2048]{1,0:T(8,128)(2,1)}), bf16[384,2048]{1,0:T(8,128)(2,1)}) %reduce-scatter.13.cloned.1.call-update) | async-done | bytes 1572880
  1353.5 164.3 %while.31 = (s32[]{:T(128)}, f32[2,6,1024,64]{2,3,1,0:T(8,128)}, f32[2,6,1024,64]{2,3,1,0:T(8,128)}, f32[2,2,6,512,64]{3,4,2,1,0:T(8,128)}, s32[2]{0:T(128)S(1)}...) while((s32[]{:T(128)}, f32[2,6,1024,64]{2,3,1,0:T(8,128)}, ...), condition=%wide.region_19.20_spmd.clone.clone, body=%wide.region_17.19_spmd.clone.sunk.clone | while | flops 4125747712 | bytes 278057216 | solution.py:253
  1367.2 13.5 select_add_fusion.7
  1380.6 18.2 multiply_reduce_fusion.10
  1398.8 17.3 multiply_convert_fusion.8
  1447.6 14.5 select_add_fusion.7
  1462.1 18.2 multiply_reduce_fusion.10
  1480.3 17.3 multiply_convert_fusion.8
  1564.6 91.7 %all-reduce.13.cloned.1.call-done = (bf16[2048,320]{0,1:T(8,128)(2,1)}, bf16[2048,320]{0,1:T(8,128)(2,1)}) async-done(((bf16[2048,320]{0,1:T(8,128)(2,1)}, bf16[2048,320]{0,1:T(8,128)(2,1)}), (bf16[2048,320]{0,1:T(8,128)(2,1)}, bf16[2048,320]{0,1:T(8,128)(2,1)})) %all-reduce.13.cloned.1.call-update) | async-done | bytes 2621456 | tf_op jit(solution)/shard_map/psum | solution.py:263
  1698.2 210.8 %all-reduce.11.cloned.1.call-done = (bf16[2048,384]{1,0:T(8,128)(2,1)}, bf16[2048,320]{0,1:T(8,128)(2,1)}, bf16[2048,320]{0,1:T(8,128)(2,1)}, bf16[1536,512]{1,0...) async-done(((bf16[2048,384]{1,0:T(8,128)(2,1)}, bf16[2048,320]{0,1:T(8,128)(2,1)}, bf16[2048,320]{0,1:T(8,128)(2,1)}, ...) | async-done | bytes 18350096 | tf_op jit(solution)/shard_map/psum | solution.py:282
  1932.8 123.0 %reduce-scatter.11.cloned.1.call-done = bf16[2048,512]{0,1:T(8,128)(2,1)} async-done(((bf16[2048,2048]{0,1:T(8,128)(2,1)}), bf16[2048,512]{0,1:T(8,128)(2,1)}) %reduce-scatter.11.cloned.1.call-update) | async-done | bytes 2097168 | tf_op jit(solution)/shard_map/reduce_scatter | solution.py:91
  2063.6 13.4 all-reduce.4
  (344 shorter events, 484.7 us)
Async XLA Ops:
  7.2 218.2 %copy-start = (bf16[2048,384]{1,0:T(8,128)(2,1)S(1)}, bf16[2048,384]{1,0:T(8,128)(2,1)}, u32[]{:S(2)}) copy-start(bf16[2048,384]{1,0:T(8,128)(2,1)} %param.23) | copy-start | bytes 4718596
  7.2 21.1 copy-start.51
  7.2 172.6 %all-gather.4.cloned.1.call-start = ((), (), s32[]{:S(2)}) async-start(), calls=%async_computation.4 | async-start | bytes 10485760 | tf_op jit(solution)/shard_map/all_gather | solution.py:79
  31.7 148.1 %copy-start.46 = (bf16[2048,320]{0,1:T(8,128)(2,1)S(1)}, bf16[2048,320]{0,1:T(8,128)(2,1)}, u32[]{:S(2)}) copy-start(bf16[2048,320]{0,1:T(8,128)(2,1)} %param.25) | copy-start | bytes 3932164
  31.8 671.7 %all-gather.6.cloned.1.call-start = ((), (), s32[]{:S(2)}) async-start(), calls=%async_computation.5 | async-start | bytes 10485760 | tf_op jit(solution)/shard_map/all_gather | solution.py:79
  31.9 155.3 %copy-start.61 = (f32[32]{0:T(128)}, f32[32]{0:T(128)S(1)}, u32[]{:S(2)}) copy-start(f32[32]{0:T(128)S(1)} %multiply_exponential_fusion) | copy-start | bytes 388
  33.2 189.6 %copy-start.53 = (s32[6]{0:T(128)}, s32[6]{0:T(128)S(1)}, u32[]{:S(2)}) copy-start(s32[6]{0:T(128)S(1)} %fusion.103) | copy-start | bytes 76
  42.7 173.5 %copy-start.19 = (f32[2,1024,64]{1,0,2:T(2,128)}, f32[2,1024,64]{1,0,2:T(2,128)S(1)}, u32[]{:S(2)}) copy-start(f32[2,1024,64]{1,0,2:T(2,128)S(1)} %get-tuple-element.373) | copy-start | bytes 1572868
  267.4 24.4 %copy-start.9 = (bf16[2,6,1024,64]{2,3,1,0:T(8,128)(2,1)S(1)}, bf16[2,6,1024,64]{2,3,1,0:T(8,128)(2,1)}, u32[]{:S(2)}) copy-start(bf16[2,6,1024,64]{2,3,1,0:T(8,128)(2,1)} %get-tuple-element.559) | copy-start | bytes 4718596 | tf_op jit(solution)/shard_map/while
  279.5 15.4 copy-start.2
  305.0 24.4 %copy-start.9 = (bf16[2,6,1024,64]{2,3,1,0:T(8,128)(2,1)S(1)}, bf16[2,6,1024,64]{2,3,1,0:T(8,128)(2,1)}, u32[]{:S(2)}) copy-start(bf16[2,6,1024,64]{2,3,1,0:T(8,128)(2,1)} %get-tuple-element.559) | copy-start | bytes 4718596 | tf_op jit(solution)/shard_map/while
  317.1 15.4 copy-start.2
  350.1 36.7 %collective-permute-start = (bf16[1,2048,384]{1,2,0:T(8,128)(2,1)}, bf16[1,2048,384]{1,2,0:T(8,128)(2,1)}, u32[]{:S(2)}, u32[]{:S(2)}) collective-permute-start(bf16[1,2048,384]{1,2,0:T(8,128)(2,1)} %broadcast_in_dim_reshape.3), channel_id=1, source_target_pairs={{0,1},{1,0},{2,3},{3,2},{4,5},{5,4},{6,7},{7,6},{8,9},{9,8},{10,11... | collective-permute-start | bytes 4718600 | tf_op jit(solution)/shard_map/ppermute | solution.py:31
  392.8 137.8 %collective-permute-start.1 = (bf16[2,2048,384]{1,2,0:T(8,128)(2,1)}, bf16[2,2048,384]{1,2,0:T(8,128)(2,1)}, u32[]{:S(2)}, u32[]{:S(2)}) collective-permute-start(bf16[2,2048,384]{1,2,0:T(8,128)(2,1)} %get-tuple-element.364), channel_id=1, source_target_pairs={{0,2},{1,3},{2,0},{3,1},{4,6},{5,7},{6,4},{7,5},{8,10},{9,11},{10,... | collective-permute-start | bytes 9437192 | tf_op jit(solution)/shard_map/ppermute | solution.py:31
  554.4 298.6 %all-gather.8.cloned.1.call-start = ((), (), s32[]{:S(2)}) async-start(), calls=%async_computation.7 | async-start | bytes 10485760 | tf_op jit(solution)/shard_map/all_gather | solution.py:203
  555.1 494.0 %reduce-scatter.9.cloned.1.call-start = ((), (), s32[]{:S(2)}) async-start(), calls=%async_computation.8 | async-start | bytes 10485760 | tf_op jit(solution)/shard_map/reduce_scatter | solution.py:91
  876.5 15.4 copy-start.69
  876.5 15.4 copy-start.73
  906.3 291.0 %reduce-scatter.7.cloned.1.call-start = ((), (), s32[]{:S(2)}) async-start(), calls=%async_computation.6 | async-start | bytes 10485760 | tf_op jit(solution)/shard_map/reduce_scatter | solution.py:199
  920.4 410.7 %reduce-scatter.13.cloned.1.call-start = ((), (), s32[]{:S(2)}) async-start(), calls=%async_computation.10 | async-start | bytes 7864320
  1219.4 436.9 %all-reduce.13.cloned.1.call-start = ((), (), s32[]{:S(2)}) async-start(), calls=%async_computation.12 | async-start | bytes 5242880 | tf_op jit(solution)/shard_map/psum | solution.py:263
  1223.0 27.5 %slice-start.6 = ((s8[8388608]{0:T(1024)(128)(4,1)}), s8[4194304]{0:T(1024)(128)(4,1)S(1)}, s32[]{:S(2)}) async-start(s8[8388608]{0:T(1024)(128)(4,1)} %bitcast.251), calls=%async_computation.19 | async-start | bytes 8388608
  1237.5 23.4 %slice-start = ((s8[6291456]{0:T(1024)(128)(4,1)}), s8[4194304]{0:T(1024)(128)(4,1)S(1)}, s32[]{:S(2)}) async-start(s8[6291456]{0:T(1024)(128)(4,1)} %bitcast.233), calls=%async_computation.13 | async-start | bytes 8388608
  1398.8 21.8 %copy-start.6 = (bf16[2,2,6,512,64]{3,4,2,1,0:T(8,128)(2,1)S(1)}, bf16[2,2,6,512,64]{3,4,2,1,0:T(8,128)(2,1)}, u32[]{:S(2)}) copy-start(bf16[2,2,6,512,64]{3,4,2,1,0:T(8,128)(2,1)} %get-tuple-element.585) | copy-start | bytes 4718596 | tf_op jit(solution)/shard_map/while
  1480.3 21.8 %copy-start.6 = (bf16[2,2,6,512,64]{3,4,2,1,0:T(8,128)(2,1)S(1)}, bf16[2,2,6,512,64]{3,4,2,1,0:T(8,128)(2,1)}, u32[]{:S(2)}) copy-start(bf16[2,2,6,512,64]{3,4,2,1,0:T(8,128)(2,1)} %get-tuple-element.585) | copy-start | bytes 4718596 | tf_op jit(solution)/shard_map/while
  1551.2 357.8 %all-reduce.11.cloned.1.call-start = ((), (), s32[]{:S(2)}) async-start(), calls=%async_computation.11 | async-start | bytes 36700160 | tf_op jit(solution)/shard_map/psum | solution.py:282
  1671.5 384.3 %reduce-scatter.11.cloned.1.call-start = ((), (), s32[]{:S(2)}) async-start(), calls=%async_computation.9 | async-start | bytes 10485760 | tf_op jit(solution)/shard_map/reduce_scatter | solution.py:91
  1928.3 127.5 %copy-start.36 = (bf16[2048,320]{0,1:T(8,128)(2,1)S(1)}, bf16[2048,320]{0,1:T(8,128)(2,1)}, u32[]{:S(2)}) copy-start(bf16[2048,320]{0,1:T(8,128)(2,1)} %get-tuple-element.349) | copy-start | bytes 3932164
  1928.3 127.5 %copy-start.44 = (f32[2048]{0:T(1024)S(1)}, f32[2048]{0:T(1024)}, u32[]{:S(2)}) copy-start(f32[2048]{0:T(1024)} %copy-done.43) | copy-start | bytes 24580
  1928.3 127.5 %copy-start.52 = (f32[512]{0:T(512)S(1)}, f32[512]{0:T(512)}, u32[]{:S(2)}) copy-start(f32[512]{0:T(512)} %param.22) | copy-start | bytes 6148
  1932.8 130.8 %copy-start.60 = (bf16[512]{0:T(512)(128)(2,1)S(1)}, bf16[512]{0:T(512)(128)(2,1)}, u32[]{:S(2)}) copy-start(bf16[512]{0:T(512)(128)(2,1)} %get-tuple-element.291) | copy-start | bytes 3076
  1932.8 158.2 %copy-start.49 = (f32[2048]{0:T(1024)S(1)}, f32[2048]{0:T(1024)}, u32[]{:S(2)}) copy-start(f32[2048]{0:T(1024)} %get-tuple-element.375) | copy-start | bytes 24580
  (69 other events, 354.6 us)
Sparse Core Ops, SparseCore 0:
  31.9 147.8 all-gather.3
  554.5 148.9 all-gather.5
  705.1 147.8 all-gather.7
  906.4 142.6 reduce-scatter.8
  1051.9 145.3 reduce-scatter.6
  1219.5 111.4 reduce-scatter.12
  1551.3 104.9 all-reduce.12
  1671.7 237.2 all-reduce.10
  1911.3 144.4 reduce-scatter.10
